TPU v7x, 32 devices: a whole 2x2x4 slice. The times are simulated.
32 devices in a mesh: gx: 4 (over y, x), gy: 8 (over z, core).
Axes of the slice: x: 2, y: 2, z: 4, core: 2. Of those that a mesh axis runs over, the one named last changes fastest.
Arguments:
- adjoint_prev: float32 [2, 20, 256, 1024], P(None, None, 'gx', 'gy'), may hold values from -2 to 2
- viscosity: float32 [20, 256, 1024], P(None, 'gx', 'gy'), may hold values from 0.5 to 4
- friction: float32 [256, 1024], P('gx', 'gy'), may hold values from 0.5 to 20
- basal_velocity: float32 [2, 256, 1024], P(None, 'gx', 'gy'), may hold values from -6 to 6
- ice_mask: int32 [256, 1024], P('gx', 'gy'), may hold values 0 or 1
- misfit: bfloat16 [32768, 2, 128], P(('gx', 'gy')), may hold values from -60 to 60
- block_tile: int32 [32768, 1], P(('gx', 'gy')), may hold values from 0 to 31; in each aligned block of 1024 rows (0 to 1023, 1024 to 2047, ...) at most 64 rows name the same one
- block_row: int32 [32768], P(('gx', 'gy')), may hold values from 0 to 63
Outputs:
- adjoint: float32 [2, 20, 256, 1024], P(None, None, 'gx', 'gy')
- gradient: float32 [256, 1024], P('gx', 'gy')
Inputs may be any that keep to these rules, and one draw needn't show every extreme that they name: `block_tile`: among the 1024 blocks of one device no tile is named more than 64 times, a bound that some block reaches.
All inputs are finite; a program needn't handle non-finite values. No bound on the sum of `ice_mask` on one device may be relied on, other than what follows from the above.
Results may differ from a plain program's by a relative error of at most 0.0003.
Values may be sent and summed in bfloat16 or wider, within the bound.
No kernel may reach another device: no remote copies, remote signals or barrier semaphores. Data moves between devices by JAX's collectives and lax.ppermute only.
A program may use at most 64 MiB of HBM per device.

v0:
```python
import functools
import math

import jax
import jax.numpy as jnp
from jax import lax
from jax.experimental import pallas as pl
from jax.experimental.pallas import tpu as pltpu
from jax.sharding import PartitionSpec as P


ITERS = 3
HALO = ITERS
GROUP = 2 * HALO
VERTICAL = 4.0

F32 = jnp.float32
BF16 = jnp.bfloat16


def omega_list(count):
    return [
        1.0 / (1.3 + 1.2 * math.cos((2 * turn_id + 1) * math.pi / (2 * count)))
        for turn_id in range(count)
    ]


def shift_up(array, axis):
    peers = lax.axis_size(axis)
    return lax.ppermute(array, axis, [(i, i + 1) for i in range(peers - 1)])


def shift_down(array, axis):
    peers = lax.axis_size(axis)
    return lax.ppermute(array, axis, [(i + 1, i) for i in range(peers - 1)])


def vmem_specs(count):
    return [pl.BlockSpec(memory_space=pltpu.VMEM) for _ in range(count)]


LEAD = 8


def stored(circle):
    return circle + 2 * LEAD


def tile_of(ref, r, step=0):
    return ref[LEAD + 8 * r + step : LEAD + 8 * (r + 1) + step, :]


def put_tile(ref, r, values, tiles):
    ref[LEAD + 8 * r : LEAD + 8 * (r + 1), :] = values
    if r == tiles - 1:
        ref[LEAD - 1 : LEAD, :] = values[7:, :]
    if r == 0:
        ref[LEAD + 8 * tiles : LEAD + 8 * tiles + 1, :] = values[:1, :]


def rows_of(r):
    return slice(8 * r, 8 * (r + 1))


def lanes_before(values, step=1):
    return pltpu.roll(values, step, 1)


def lanes_after(values, step=1):
    return pltpu.roll(values, values.shape[1] - step, 1)


def lane_index(shape):
    return lax.broadcasted_iota(jnp.int32, shape, len(shape) - 1)


def extend(slot, values, above, below, plane):
    rows = values.shape[0]
    circle = slot.shape[0]
    first = HALO * plane
    slot[:rows, :] = values
    slot[rows : rows + HALO, :] = below[first : first + HALO, :]
    slot[rows + HALO : circle - HALO, :] = jnp.zeros((8 - 2 * HALO, values.shape[1]), F32)
    slot[circle - HALO : circle, :] = above[first : first + HALO, :]
    return slot


def in_turn(tiles, front, back, count=None):
    done = {tiles - 1: front(tiles - 1), 0: front(0)}
    count = tiles if count is None else count
    for r in range(1, tiles - 1):
        done[r] = front(r)
        back(r - 1, done[r - 1])
    for r in range(tiles - 2, count):
        back(r, done[r])


def edge_kernel(layers, adj_lo, adj_hi, eta_lo, eta_hi, fr_lo, fr_hi, ice_lo, ice_hi, lo, hi):
    for adj, eta, fr, ice, out, at in (
        (adj_lo, eta_lo, fr_lo, ice_lo, lo, 0),
        (adj_hi, eta_hi, fr_hi, ice_hi, hi, 8 - HALO),
    ):
        rows = slice(at, at + HALO)
        covered = ice[rows, :] > 0
        for plane in range(2 * layers):
            values = jnp.where(covered, adj[plane // layers, plane % layers, rows, :], 0.0)
            out[HALO * plane : HALO * (plane + 1), :] = values
        for layer in range(layers):
            values = eta[layer, rows, :]
            first = HALO * (2 * layers + layer)
            out[first : first + HALO, :] = jnp.where(covered, values, -values)
        first = HALO * 3 * layers
        out[first : first + HALO, :] = fr[rows, :]


def edge_rows(adjoint, viscosity, friction, ice_mask):
    _, layers, rows, cols = adjoint.shape
    last = rows // 8 - 1
    length = -(-HALO * (3 * layers + 1) // 8) * 8

    def pair(block, index):
        return [
            pl.BlockSpec(block, functools.partial(index, 0)),
            pl.BlockSpec(block, functools.partial(index, last)),
        ]

    specs = pair((2, layers, 8, cols), lambda r, i: (0, 0, r, 0))
    specs += pair((layers, 8, cols), lambda r, i: (0, r, 0))
    specs += pair((8, cols), lambda r, i: (r, 0))
    specs += pair((8, cols), lambda r, i: (r, 0))
    return pl.pallas_call(
        functools.partial(edge_kernel, layers),
        grid=(1,),
        in_specs=specs,
        out_specs=[pl.BlockSpec((length, cols), lambda i: (0, 0))] * 2,
        out_shape=[jax.ShapeDtypeStruct((length, cols), F32)] * 2,
        compiler_params=pltpu.CompilerParams(vmem_limit_bytes=60 << 20),
        name="edge_rows",
    )(adjoint, adjoint, viscosity, viscosity, friction, friction, ice_mask, ice_mask)


def column_kernel(layers, adj, eta, fr, ice, above, below, packed, work):
    rows, cols = fr.shape
    circle = rows + 8
    lane_layer = lane_index((circle, cols)) // GROUP
    covered = ice[...] > 0

    def gather(total, values, layer):
        return jnp.where(
            lane_layer == layer, pltpu.roll(values, (HALO + GROUP * layer) % cols, 1), total
        )

    for field in range(3):
        total = jnp.zeros((circle, cols), F32)
        for layer in range(layers):
            if field == 2:
                values = jnp.where(covered, eta[layer], -eta[layer])
            else:
                values = jnp.where(covered, adj[field, layer], 0.0)
            slot = extend(work.at[layer % 2], values, above, below, field * layers + layer)
            total = gather(total, slot[...], layer)
        if field == 2:
            slot = extend(work.at[layers % 2], fr[...], above, below, 3 * layers)
            total = gather(total, slot[...], layers)
        packed[field] = total


def edge_columns(adjoint, viscosity, friction, ice_mask, above, below):
    _, layers, rows, cols = adjoint.shape
    circle = rows + 8
    return pl.pallas_call(
        functools.partial(column_kernel, layers),
        in_specs=vmem_specs(6),
        out_specs=pl.BlockSpec(memory_space=pltpu.VMEM),
        out_shape=jax.ShapeDtypeStruct((3, circle, cols), F32),
        scratch_shapes=[pltpu.VMEM((2, circle, cols), F32)],
        compiler_params=pltpu.CompilerParams(vmem_limit_bytes=4 << 20),
        name="edge_columns",
    )(adjoint, viscosity, friction, ice_mask, above, below)


def keep_of(omega):
    return (1.0 - omega) / omega


def cross_factors(c, e):
    half, quarter = 0.5 * e, 0.25 * e
    return (half, quarter) if c == 0 else (quarter, half)


def gathered(c, e, sum_x, sum_y, along_x, along_y):
    strong, weak = (0, 1) if c == 0 else (1, 0)
    sums, alongs = (sum_x, sum_y), (along_x, along_y)
    return e * (sums[strong] + 0.25 * sums[weak]) + (alongs[strong] + 0.25 * alongs[weak])


def strip_planes(strip, signed, layers, scratch):
    circle, cols = signed.shape
    tiles = circle // 8
    lane = lane_index((8, cols))
    inside = lane < GROUP * layers
    bottom = inside & (lane >= GROUP * (layers - 1))
    ends = jnp.where(bottom | (lane < GROUP), 1.0, 2.0)
    for r in range(tiles):
        e = jnp.where(inside, jnp.abs(signed[rows_of(r)]), 0.0)
        put_tile(scratch, r, e, tiles)
        strip[0, rows_of(r), :] = e
    for r in range(tiles):
        e = tile_of(scratch, r)
        here = signed[rows_of(r)]
        z_low, z_high = lanes_before(e, GROUP), lanes_after(e, GROUP)
        strip[3, rows_of(r), :] = e + z_low
        strip[4, rows_of(r), :] = e + z_high
        pair = inverse_pair(
            e,
            tile_of(scratch, r, -1) + tile_of(scratch, r, 1),
            lanes_before(e) + lanes_after(e),
            z_low + z_high,
            ends,
            jnp.where(bottom, lanes_after(here, GROUP), 0.0),
            jnp.where(inside & (here > 0.0), 2.0, 0.0),
        )
        strip[1, rows_of(r), :], strip[2, rows_of(r), :] = pair


def strip_sweep(strip, fields, news, keep, work, source=None):
    tiles = strip.shape[1] // 8

    def front(r):
        e = strip[0, rows_of(r), :]
        parts = []
        for c in range(2):
            f = tile_of(fields.at[c], r)
            y_low, y_high = lanes_before(f), lanes_after(f)
            x_low, x_high = tile_of(fields.at[c], r, -1), tile_of(fields.at[c], r, 1)
            wg, wh = cross_factors(c, e)
            part = dict(f=f, p=e * f, g=wg * (y_high - y_low), h=wh * (x_high - x_low))
            part.update(sum_x=x_low + x_high, sum_y=y_low + y_high)
            parts.append(part)
        for c in range(2):
            p, g = parts[c]["p"], parts[1 - c]["g"]
            put_tile(work.at[c, 0], r, p + g, tiles)
            put_tile(work.at[c, 1], r, p - g, tiles)
        return e, parts

    def back(r, state):
        e, parts = state
        for c in range(2):
            mine = parts[c]
            f, p, h = mine["f"], mine["p"], parts[1 - c]["h"]
            along_x = tile_of(work.at[c, 0], r, 1) + tile_of(work.at[c, 1], r, -1)
            along_y = lanes_after(p + h) + lanes_before(p - h)
            total = gathered(c, e, mine["sum_x"], mine["sum_y"], along_x, along_y)
            total = total + strip[3, rows_of(r), :] * lanes_before(f, GROUP)
            total = total + strip[4, rows_of(r), :] * lanes_after(f, GROUP)
            if source is not None:
                total = total + source(c, r)
            put_tile(news.at[c], r, keep * f + strip[1 + c, rows_of(r), :] * total, tiles)

    in_turn(tiles, front, back)


def join_sides(sides, left, right, column):
    for r in range(sides.shape[1] // 8):
        for c in range(2):
            both = jnp.where(column == HALO, tile_of(left.at[c], r), tile_of(right.at[c], r))
            sides[c, rows_of(r), :] = both


def join_edges(edges, strips, left, right, column, tiles):
    for r in range(tiles):
        sums = []
        for strip, fields, sign in ((strips[0], left, -1.0), (strips[1], right, 1.0)):
            e = strip[0, rows_of(r), :]
            p, h = [], []
            for c in range(2):
                _, wh = cross_factors(c, e)
                step = tile_of(fields.at[c], r, 1) - tile_of(fields.at[c], r, -1)
                p.append(e * tile_of(fields.at[c], r))
                h.append((sign * wh) * step)
            sums.append([p[c] + h[1 - c] for c in range(2)])
        before = column == HALO - 1
        for c in range(2):
            f = jnp.where(before, tile_of(left.at[c], r), tile_of(right.at[c], r))
            edges[0, c, rows_of(r), :] = f
            edges[1, c, rows_of(r), :] = jnp.where(before, sums[0][c], sums[1][c])


def plane_sweep(k, lane, eta, fields, products, scale, keep, work, put, sides, edges, source=None):
    tiles = scale.shape[2] // 8
    count = tiles if edges is None else tiles - 1
    cols = lane.shape[1]
    back_by = cols - (GROUP * k + HALO)
    first, last = lane == 0, lane == cols - 1
    at_side = first | last

    def front(r):
        e = tile_of(eta.at[k + 1], r)
        parts = []
        for c in range(2):
            plane = fields.at[c, k + 1]
            f = tile_of(plane, r)
            low = high = f
            if edges is not None:
                edge = pltpu.roll(edges[0, c, rows_of(r), :], back_by, 1)
                low, high = jnp.where(last, edge, f), jnp.where(first, edge, f)
            y_low, y_high = lanes_before(low), lanes_after(high)
            x_low, x_high = tile_of(plane, r, -1), tile_of(plane, r, 1)
            wg, wh = cross_factors(c, e)
            part = dict(f=f, g=wg * (y_high - y_low), h=wh * (x_high - x_low))
            part.update(sum_x=x_low + x_high, sum_y=y_low + y_high)
            part.update(p=tile_of(products.at[c, k + 1], r))
            parts.append(part)
        for c in range(2):
            p, g = parts[c]["p"], parts[1 - c]["g"]
            put_tile(work.at[c, 0], r, p + g, tiles)
            put_tile(work.at[c, 1], r, p - g, tiles)
        return e, parts

    def back(r, state):
        e, parts = state
        for c in range(2):
            mine = parts[c]
            p, h = mine["p"], parts[1 - c]["h"]
            low, high = p - h, p + h
            if edges is not None:
                edge = pltpu.roll(edges[1, c, rows_of(r), :], back_by, 1)
                low, high = jnp.where(last, edge, low), jnp.where(first, edge, high)
            along_x = tile_of(work.at[c, 0], r, 1) + tile_of(work.at[c, 1], r, -1)
            along_y = lanes_before(low) + lanes_after(high)
            sum_z = tile_of(fields.at[c, k], r) + tile_of(fields.at[c, k + 2], r)
            p_z = tile_of(products.at[c, k], r) + tile_of(products.at[c, k + 2], r)
            sums = [mine["sum_x"], mine["sum_y"]]
            alongs = [along_x, along_y]
            sums[c], alongs[c] = sums[c] + sum_z, alongs[c] + p_z
            total = gathered(c, e, sums[0], sums[1], alongs[0], alongs[1])
            if source is not None:
                total = total + source(c, r)
            new = keep * mine["f"] + scale[c, k, rows_of(r), :] * total
            if edges is None:
                side = pltpu.roll(sides[c, rows_of(r), :], back_by, 1)
                new = jnp.where(at_side, side, new)
            put(c, k, r, e, new)

    in_turn(tiles, front, back, count)


def inverse_pair(e, e_x, e_y, e_z, ends, basal, cover):
    double = 2.0 * e
    both_x, both_y = e_x + double, e_y + double
    vertical = (VERTICAL / 2) * (e_z + ends * e) + basal
    first = 2.0 * both_x + 0.5 * both_y + vertical
    second = 0.5 * both_x + 2.0 * both_y + vertical
    inverse = cover / jnp.where(cover > 0.0, first * second, 1.0)
    return inverse * second, inverse * first


UNROLL = 1


def over_layers(layers, body):
    def some(i, carry):
        for slot in range(UNROLL):
            body(UNROLL * i + slot, slot)
        return carry

    lax.fori_loop(0, layers // UNROLL, some, 0)
    for k in range(layers // UNROLL * UNROLL, layers):
        body(k, k % UNROLL)


def sweep_kernel(
    layers,
    adj, eta_in, fr, ice, above, below, packed, packed_left, packed_right, basal_velocity,
    out, gradient, carry_out,
    fields, products, eta, cover, friction, eta_edge, sides, edges,
    strip_fields, strip_work, plane_work, circle_work, scale, strips,
):
    circle, cols = friction.shape
    tiles = circle // 8
    lane = lane_index((8, cols))
    column = lane % GROUP
    omegas = omega_list(ITERS)

    whole_column = lane_index((circle, cols)) % GROUP
    for side in range(2):
        values = []
        for field in range(3):
            own = packed[field]
            if side == 0:
                values.append(jnp.where(whole_column < HALO, packed_left[field], own))
            else:
                values.append(jnp.where(whole_column < HALO, own, packed_right[field]))
        strip_planes(strips.at[side], values[2], layers, strip_work.at[side, 0, 0])
        for c in range(2):
            for r in range(tiles):
                put_tile(strip_fields.at[0, side, c], r, values[c][rows_of(r)], tiles)
    for r in range(tiles):
        both = jnp.where(
            column == HALO - 1, strips[0, 0, rows_of(r), :], strips[1, 0, rows_of(r), :]
        )
        eta_edge[rows_of(r), :] = both

    zero = jnp.zeros((stored(circle), cols), F32)
    for end in (0, layers + 1):
        eta[end] = zero
        for half in range(2):
            for c in range(2):
                fields[half, c, end] = zero
                products[half, c, end] = zero
    covered = ice[...] > 0
    extend(friction, fr[...], above, below, 3 * layers)
    for layer in range(layers):
        slot = circle_work.at[layer % 2]
        values = eta_in[layer]
        signed = slot.at[0]
        extend(signed, jnp.where(covered, values, -values), above, below, 2 * layers + layer)
        for c in range(2):
            values = jnp.where(covered, adj[c, layer], 0.0)
            extend(slot.at[1 + c], values, above, below, c * layers + layer)
        for r in range(tiles):
            here = signed[rows_of(r), :]
            if layer == 0:
                cover[rows_of(r), :] = jnp.where(here > 0.0, 2.0, 0.0)
            e = jnp.abs(here)
            put_tile(eta.at[layer + 1], r, e, tiles)
            for c in range(2):
                f = slot[1 + c, rows_of(r), :]
                put_tile(fields.at[0, c, layer + 1], r, f, tiles)
                products[0, c, layer + 1, LEAD + 8 * r : LEAD + 8 * (r + 1), :] = e * f

    def weigh(k, slot):
        is_end = (k == 0) | (k == layers - 1)
        ends = jnp.where(is_end, 1.0, 2.0)
        lowest = jnp.where(k == layers - 1, 1.0, 0.0)
        plane = eta.at[k + 1]
        for r in range(tiles):
            e = tile_of(plane, r)
            edge = pltpu.roll(eta_edge[rows_of(r), :], cols - (GROUP * k + HALO), 1)
            e_y = lanes_before(jnp.where(lane == cols - 1, edge, e))
            e_y = e_y + lanes_after(jnp.where(lane == 0, edge, e))
            pair = inverse_pair(
                e,
                tile_of(plane, r, -1) + tile_of(plane, r, 1),
                e_y,
                tile_of(eta.at[k], r) + tile_of(eta.at[k + 2], r),
                ends,
                lowest * friction[rows_of(r), :],
                cover[rows_of(r), :],
            )
            scale[0, k, rows_of(r), :], scale[1, k, rows_of(r), :] = pair

    over_layers(layers, weigh)

    total = math.prod(omegas)
    for turn, omega in enumerate(omegas):
        final = turn == ITERS - 1
        half = turn % 2
        olds = strip_fields.at[half]
        news = strip_fields.at[1 - half]
        keep = keep_of(omega)
        if final:
            join_edges(
                edges, (strips.at[0], strips.at[1]), olds.at[0], olds.at[1], column, tiles - 1 + 1
            )
        else:
            for side in range(2):
                strip_sweep(
                    strips.at[side], olds.at[side], news.at[side], keep, strip_work.at[side]
                )
            join_sides(sides, news.at[0], news.at[1], column)

        def put(c, k, r, e, new, final=final, half=half):
            if final:
                out[c, k, rows_of(r), :] = total * new
            else:
                put_tile(fields.at[1 - half, c, k + 1], r, new, tiles)
                products[1 - half, c, k + 1, LEAD + 8 * r : LEAD + 8 * (r + 1), :] = e * new

        def sweep(k, slot, final=final, half=half, keep=keep, put=put):
            plane_sweep(
                k, lane, eta, fields.at[half], products.at[half], scale, keep,
                plane_work.at[slot], put, sides, edges if final else None,
            )

        over_layers(layers, sweep)

    flow = basal_velocity[0] * out[0, layers - 1] + basal_velocity[1] * out[1, layers - 1]
    gradient[...] = jnp.where(covered, -fr[...] * flow, 0.0)
    for i in range(2):
        for k in range(ITERS):
            carry_out[i, k] = scale[i, k]
        for k in range(3):
            carry_out[i, ITERS + k] = strips[i, k]
        for k in range(2):
            carry_out[i, ITERS + 3 + k] = eta[2 * i + k + 1, LEAD : LEAD + circle, :]


def free_sweeps(adjoint, viscosity, friction, ice_mask, edges, packed, basal_velocity):
    _, layers, rows, cols = adjoint.shape
    circle = rows + 8
    plane = (circle, cols)
    kept = (stored(circle), cols)
    stack = (layers + 2,) + kept
    return pl.pallas_call(
        functools.partial(sweep_kernel, layers),
        in_specs=vmem_specs(10),
        out_specs=vmem_specs(3),
        out_shape=[
            jax.ShapeDtypeStruct(adjoint.shape, F32),
            jax.ShapeDtypeStruct((rows, cols), F32),
            jax.ShapeDtypeStruct((2, ITERS + 5) + plane, F32),
        ],
        scratch_shapes=[
            pltpu.VMEM((2, 2) + stack, F32),
            pltpu.VMEM((2, 2) + stack, F32),
            pltpu.VMEM(stack, F32),
            pltpu.VMEM(plane, F32),
            pltpu.VMEM(plane, F32),
            pltpu.VMEM(plane, F32),
            pltpu.VMEM((2,) + plane, F32),
            pltpu.VMEM((2, 2) + plane, F32),
            pltpu.VMEM((2, 2, 2) + kept, F32),
            pltpu.VMEM((2, 2, 2) + kept, F32),
            pltpu.VMEM((UNROLL, 2, 2) + kept, F32),
            pltpu.VMEM((2, 3) + plane, F32),
            pltpu.VMEM((2, layers) + plane, F32),
            pltpu.VMEM((2, 5) + plane, F32),
        ],
        compiler_params=pltpu.CompilerParams(vmem_limit_bytes=24 << 20),
        cost_estimate=pl.CostEstimate(
            flops=200_000_000, transcendentals=0, bytes_accessed=8_000_000
        ),
        name="free_sweeps",
    )(adjoint, viscosity, friction, ice_mask, *edges, *packed, basal_velocity)


EXTRA = 12
CORNER = 16


def pack_kernel(capacity, tile_in, row_in, misfit_in, out, keys_out, counts_out,
                tile, row, misfit, slot_vector, slot, sems):
    copies = [
        pltpu.make_async_copy(source, target, sems.at[i])
        for i, (source, target) in enumerate(
            ((tile_in, tile), (row_in, row), (misfit_in, misfit))
        )
    ]
    for copy in copies:
        copy.start()
    turns, lanes = tile.shape
    devices = keys_out.shape[0]
    device = lax.broadcasted_iota(jnp.int32, (devices, lanes), 0)
    at_row = lax.broadcasted_iota(jnp.int32, (lanes, lanes), 0)
    at_lane = lax.broadcasted_iota(jnp.int32, (lanes, lanes), 1)
    earlier = jnp.where(at_row < at_lane, 1.0, 0.0).astype(BF16)
    copies[0].wait()
    seen = jnp.zeros((devices, 1), F32)
    onehots, ranks = [], []
    for turn in range(turns):
        target = tile[turn : turn + 1, :]
        onehot = jnp.where(device == target, 1.0, 0.0)
        before = jnp.dot(onehot.astype(BF16), earlier, preferred_element_type=F32) + seen
        rank = jnp.sum(onehot * before, axis=0, keepdims=True).astype(jnp.int32)
        slot_vector[turn : turn + 1, :] = target * capacity + rank
        seen = seen + jnp.sum(onehot, axis=1, keepdims=True)
        onehots.append(onehot)
        ranks.append(rank)
    copy = pltpu.make_async_copy(slot_vector, slot, sems.at[3])
    copy.start()
    counts_out[...] = jnp.broadcast_to(seen, counts_out.shape)
    copies[1].wait()
    keys = jnp.zeros((devices, lanes), F32)
    for turn in range(turns):
        named = onehots[turn] * (row[turn : turn + 1, :] + 1).astype(F32)
        place = jnp.where(at_row // 2 == ranks[turn], 1.0, 0.0).astype(BF16)
        keys = keys + lax.dot_general(
            named.astype(BF16), place, (((1,), (1,)), ((), ())), preferred_element_type=F32
        )
    keys_out[...] = keys
    copies[2].wait()
    copy.wait()

    def place_row(turn, carry):
        for i in range(lanes):
            out[slot[turn, i]] = misfit[turn * lanes + i]
        return carry

    lax.fori_loop(0, turns, place_row, 0)


def pack_blocks(misfit, block_tile, block_row, devices, capacity):
    count, _, cols = misfit.shape
    grid_shape = (count // cols, cols)
    return pl.pallas_call(
        functools.partial(pack_kernel, capacity),
        in_specs=[pl.BlockSpec(memory_space=pltpu.HBM)] * 3,
        out_specs=vmem_specs(3),
        out_shape=[
            jax.ShapeDtypeStruct((devices * capacity, 2, cols), BF16),
            jax.ShapeDtypeStruct((devices, cols), F32),
            jax.ShapeDtypeStruct((devices, cols), F32),
        ],
        scratch_shapes=[
            pltpu.VMEM(grid_shape, jnp.int32),
            pltpu.VMEM(grid_shape, jnp.int32),
            pltpu.VMEM(misfit.shape, BF16),
            pltpu.VMEM(grid_shape, jnp.int32),
            pltpu.SMEM(grid_shape, jnp.int32),
            pltpu.SemaphoreType.DMA((4,)),
        ],
        compiler_params=pltpu.CompilerParams(vmem_limit_bytes=4 << 20),
        name="pack_blocks",
    )(block_tile.reshape(grid_shape), block_row.reshape(grid_shape), misfit)


def wanted_of(keys, rows):
    odd = lax.broadcasted_iota(jnp.int32, keys.shape, 1) % 2
    return jnp.where(keys > 0.0, keys - 1.0 + odd.astype(F32) * rows, -1.0)


def halves(values):
    high = values.astype(BF16).astype(F32)
    return jnp.concatenate([high, values - high], axis=0)


def bundle_kernel(devices, across, capacity, rows, slots, keys, counts, out, upper, lower, column):
    lanes = slots.shape[1]
    span = 2 * capacity
    place = span + 2 * EXTRA
    at_row = lax.broadcasted_iota(jnp.int32, (span, lanes), 0).astype(F32)
    line = lax.broadcasted_iota(jnp.int32, (8, lanes), 0)
    lane = lax.broadcasted_iota(jnp.int32, (8, lanes), 1)
    ends = jnp.where(line < 4, rows - 2, 0) + (line // 2 % 2) * rows + line % 2
    ends = ends[:, :span].astype(F32)
    pick = (line == 1) & (lane == lanes - 2) | (line == 2) & (lane == lanes - 1)
    pick = pick | (line == 3) & (lane == 0) | (line == 4) & (lane == 1)
    pick = jnp.where(pick, 1.0, 0.0).astype(BF16)
    for t in range(devices):
        used = 2.0 * counts[t : t + 1, :]
        block = slots[span * t : span * (t + 1), :].astype(F32)
        block = jnp.where(at_row < used, block, 0.0).astype(BF16)
        out[place * t : place * t + span, :] = block
        wanted = wanted_of(keys[t : t + 1, :], rows)[:, :span]
        select = jnp.where(ends == wanted, 1.0, 0.0).astype(BF16)
        found = jnp.dot(select, block, preferred_element_type=F32)
        upper[t] = halves(found[:4])
        lower[t] = halves(found[4:])
        side = lax.dot_general(
            pick, block, (((1,), (1,)), ((), ())), preferred_element_type=F32
        )
        if span < lanes:
            side = jnp.concatenate([side, jnp.zeros((8, lanes - span), F32)], axis=1)
        column[t] = side
    zero_row = jnp.zeros((1, lanes), F32)
    zero_edge = jnp.zeros((8, lanes), F32)
    for t in range(devices):
        has_left, has_right = t % across > 0, t % across < across - 1
        has_above, has_below = t >= across, t < devices - across
        above = upper[t - across] if has_above else zero_edge
        below = lower[t + across] if has_below else zero_edge
        corner = zero_edge
        for near, there, edge, first in (
            (t - across, has_above, upper, 0),
            (t + across, has_below, lower, 8),
        ):
            if there and has_left:
                value = pltpu.roll(edge[near - 1], HALO + first, 1)
                corner = jnp.where((lane == first + 1) | (lane == first + 2), value, corner)
            if there and has_right:
                value = pltpu.roll(edge[near + 1], HALO + first, 1)
                corner = jnp.where((lane == first + 3) | (lane == first + 4), value, corner)
        corner = pltpu.roll(corner, 0, 1, stride=CORNER, stride_axis=0)
        corner = jnp.sum(corner, axis=0, keepdims=True)
        key_left = keys[t - 1 : t, :] if has_left else zero_row
        key_right = keys[t + 1 : t + 2, :] if has_right else zero_row
        left = column[t - 1, 1:3, :] if has_left else zero_edge[:2]
        right = column[t + 1, 3:5, :] if has_right else zero_edge[:2]
        head = jnp.concatenate(
            [keys[t : t + 1, :], key_left, key_right, corner, left, right], axis=0
        )
        extra = jnp.concatenate([head, above, below], axis=0).astype(BF16)
        out[place * t + span : place * (t + 1), :] = extra


def bundle_blocks(slots, keys, counts, across, capacity, rows):
    devices, cols = keys.shape
    length = devices * 2 * (capacity + EXTRA)
    edge = pltpu.VMEM((devices, 8, cols), F32)
    return pl.pallas_call(
        functools.partial(bundle_kernel, devices, across, capacity, rows),
        in_specs=vmem_specs(3),
        out_specs=pl.BlockSpec(memory_space=pltpu.VMEM),
        out_shape=jax.ShapeDtypeStruct((length, cols), BF16),
        scratch_shapes=[edge, edge, edge],
        compiler_params=pltpu.CompilerParams(vmem_limit_bytes=8 << 20),
        name="bundle_blocks",
    )(slots, keys, counts)


def source_of(devices, capacity, rows, got, source, beside):
    lanes = got.shape[1]
    circle = rows + 8
    span = 2 * capacity
    place = span + 2 * EXTRA
    group = max(1, lanes // span)
    at_row = lax.broadcasted_iota(jnp.int32, (2 * rows, lanes), 0).astype(F32)
    line = lax.broadcasted_iota(jnp.int32, (8, lanes), 0)
    total = jnp.zeros((2 * rows, lanes), F32)
    side = jnp.zeros((2 * rows, 8), F32)
    extra_sum = jnp.zeros((2 * EXTRA, lanes), F32)
    contract = (((1,), (1,)), ((), ()))
    pair_pick, pair_block = [], []
    for first in range(0, devices, group):
        keys, blocks = None, []
        for q in range(group):
            start = (first + q) * place
            extra = got[start + span : start + place, :].astype(F32)
            extra_sum = extra_sum + extra
            head = pltpu.roll(extra[:8], q * span, 1) if q else extra[:8]
            keys = head if keys is None else keys + head
            blocks.append(got[start : start + span, :])
        wanted = wanted_of(keys[:3], rows)
        block = blocks[0] if group == 1 else jnp.concatenate(blocks, axis=0)
        picks = [
            jnp.where(at_row == wanted[i : i + 1], 1.0, 0.0).astype(BF16) for i in range(3)
        ]
        pair_pick.append(picks[0])
        pair_block.append(block)
        if len(pair_pick) == 2:
            pick, block = jnp.concatenate(pair_pick, axis=1), jnp.concatenate(pair_block, axis=0)
            total = total + jnp.dot(pick, block, preferred_element_type=F32)
            pair_pick, pair_block = [], []
        low = jnp.where((line == 1) | (line == 2), pltpu.roll(keys, 5, 0), 0.0).astype(BF16)
        high = jnp.where((line == 3) | (line == 4), pltpu.roll(keys, 5, 0), 0.0).astype(BF16)
        pick, both = jnp.concatenate(picks[1:], axis=1), jnp.concatenate([low, high], axis=1)
        side = side + lax.dot_general(pick, both, contract, preferred_element_type=F32)
    above = extra_sum[8:12] + extra_sum[12:16]
    below = extra_sum[16:20] + extra_sum[20:24]
    lane = lax.broadcasted_iota(jnp.int32, (8, lanes), 1)
    corner = jnp.where(lane // CORNER == 7 - line, extra_sum[3:4], 0.0)
    corner = pltpu.roll(corner, lanes - 7 * CORNER, 1, stride=CORNER, stride_axis=0)
    corner = corner[:4] + corner[4:]
    corner = jnp.concatenate([corner[3 - i : 4 - i] for i in range(4)], axis=0)
    corner_below = pltpu.roll(corner, lanes - 8, 1)
    side = jnp.concatenate([side, jnp.zeros((2 * rows, lanes - 8), F32)], axis=1)
    gap = jnp.zeros((4, lanes), F32)
    for c in range(2):
        for target, inner, after, before in (
            (source, total, below, above),
            (beside, side, corner_below, corner),
        ):
            target[c, :rows, :] = inner[c * rows : (c + 1) * rows]
            target[c, rows : rows + 2, :] = after[2 * c : 2 * c + 2]
            target[c, rows + 2 : circle - 2, :] = gap
            target[c, circle - 2 : circle, :] = before[2 * c : 2 * c + 2]


def response_kernel(
    devices, capacity,
    got, scale, adj_in,
    out, source, beside, fields, products, eta, sides, edges,
    drives, strip_fields, strip_work, plane_work, strips,
):
    circle, cols = source.shape[1:]
    rows = out.shape[2]
    tiles = circle // 8
    source_of(devices, capacity, rows, got, source, beside)
    lane = lane_index((8, cols))
    column = lane % GROUP
    omegas = omega_list(ITERS)
    zero = jnp.zeros((stored(circle), cols), F32)
    top = lane < GROUP
    for side in range(2):
        for r in range(tiles):
            e = scale[side, ITERS, rows_of(r), :]
            for i in range(3):
                strips[side, i, rows_of(r), :] = scale[side, ITERS + i, rows_of(r), :]
            strips[side, 3, rows_of(r), :] = e + lanes_before(e, GROUP)
            strips[side, 4, rows_of(r), :] = e + lanes_after(e, GROUP)
    for k in range(2):
        for half in range(2):
            for c in range(2):
                fields[half, c, 0] = zero
                products[half, c, 0] = zero
                fields[half, c, 2 + half + k] = zero
                products[half, c, 2 + half + k] = zero
    eta[0] = zero
    for k in range(ITERS + 1):
        for r in range(tiles):
            put_tile(eta.at[k + 1], r, scale[k // 2, ITERS + 3 + k % 2, rows_of(r), :], tiles)

    def put_strip(turn, side, c, r, value):
        put_tile(strip_fields.at[turn % 2, side, c], r, value, tiles)

    for r in range(tiles):
        e = tile_of(eta.at[1], r)
        for c in range(2):
            drive = 0.5 * source[c, rows_of(r), :]
            source[c, rows_of(r), :] = drive
            f = scale[c, 0, rows_of(r), :] * drive
            put_tile(fields.at[0, c, 1], r, f, tiles)
            products[0, c, 1, LEAD + 8 * r : LEAD + 8 * (r + 1), :] = e * f
            own = lanes_before(drive, HALO)
            near = 0.5 * beside[c, rows_of(r), :]
            for side in range(2):
                pair = (near, own) if side == 0 else (own, near)
                both = jnp.where(top, jnp.where(column < HALO, pair[0], pair[1]), 0.0)
                drives[side, c, rows_of(r), :] = both
                put_strip(0, side, c, r, strips[side, 1 + c, rows_of(r), :] * both)

    reach = omegas[0]
    for turn in range(1, ITERS):
        final = turn == ITERS - 1
        half = turn - 1
        part = 1.0 / reach
        keep = keep_of(omegas[turn])
        olds, news = strip_fields.at[half % 2], strip_fields.at[turn % 2]
        if final:
            join_edges(
                edges, (strips.at[0], strips.at[1]), olds.at[0], olds.at[1], column, tiles
            )
        else:
            for side in range(2):
                strip_sweep(
                    strips.at[side], olds.at[side], news.at[side], keep, strip_work.at[side],
                    lambda c, r, side=side: part * drives[side, c, rows_of(r), :],
                )
            join_sides(sides, news.at[0], news.at[1], column)
        after = reach * omegas[turn]

        def put(c, k, r, e, new, final=final, turn=turn, after=after):
            if final:
                out[c, k, rows_of(r), :] = adj_in[c, k, rows_of(r), :] + after * new
            else:
                put_tile(fields.at[turn, c, k + 1], r, new, tiles)
                products[turn, c, k + 1, LEAD + 8 * r : LEAD + 8 * (r + 1), :] = e * new

        for k in range(turn + 1):
            drive = None
            if k == 0:
                drive = lambda c, r, part=part: part * source[c, rows_of(r), :]
            plane_sweep(
                k, lane, eta, fields.at[half], products.at[half], scale, keep,
                plane_work.at[k % 2], put, sides, edges if final else None, drive,
            )
        reach = after


def add_response(got, devices, capacity, carry, adjoint):
    circle, cols = carry.shape[2:]
    _, _, rows, _ = adjoint.shape
    plane = (circle, cols)
    kept = (stored(circle), cols)
    top = pl.BlockSpec((2, ITERS, rows, cols), lambda i: (0, 0, 0, 0))

    def whole(array):
        return pl.BlockSpec(array.shape, lambda i, n=array.ndim: (0,) * n)

    return pl.pallas_call(
        functools.partial(response_kernel, devices, capacity),
        grid=(1,),
        in_specs=[whole(got), whole(carry), top],
        out_specs=top,
        out_shape=jax.ShapeDtypeStruct(adjoint.shape, F32),
        scratch_shapes=[
            pltpu.VMEM((2,) + plane, F32),
            pltpu.VMEM((2,) + plane, F32),
            pltpu.VMEM((2, 2, ITERS + 2) + kept, F32),
            pltpu.VMEM((2, 2, ITERS + 2) + kept, F32),
            pltpu.VMEM((ITERS + 2,) + kept, F32),
            pltpu.VMEM((2,) + plane, F32),
            pltpu.VMEM((2, 2) + plane, F32),
            pltpu.VMEM((2, 2) + plane, F32),
            pltpu.VMEM((2, 2, 2) + kept, F32),
            pltpu.VMEM((2, 2, 2) + kept, F32),
            pltpu.VMEM((2, 2, 2) + kept, F32),
            pltpu.VMEM((2, 5) + plane, F32),
        ],
        input_output_aliases={2: 0},
        compiler_params=pltpu.CompilerParams(vmem_limit_bytes=12 << 20),
        name="add_response",
    )(got, carry, adjoint)


def on_device(
    adjoint_prev, viscosity, friction, basal_velocity, ice_mask, misfit, block_tile, block_row
):
    devices = lax.axis_size("gx") * lax.axis_size("gy")
    layers, rows, cols = adjoint_prev.shape[1:]
    capacity = 2 * misfit.shape[0] // devices
    assert layers > 2 * ITERS and GROUP * (layers + 1) <= cols and rows % 8 == 0
    assert devices % (cols // capacity) == 0 and 2 * capacity <= cols and cols % (2 * capacity) == 0 and misfit.shape[0] % cols == 0

    edge_low, edge_high = edge_rows(adjoint_prev, viscosity, friction, ice_mask)
    above = shift_up(edge_high, "gx")
    below = shift_down(edge_low, "gx")
    slots, keys, counts = pack_blocks(misfit, block_tile, block_row, devices, capacity)
    sent = bundle_blocks(
        slots.reshape(-1, cols), keys, counts, lax.axis_size("gy"), capacity, rows
    )
    got = lax.all_to_all(
        sent.reshape(devices, -1, cols), ("gx", "gy"), split_axis=0, concat_axis=0, tiled=True
    )
    packed = edge_columns(adjoint_prev, viscosity, friction, ice_mask, above, below)
    left = shift_up(packed, "gy")
    right = shift_down(packed, "gy")
    adjoint, gradient, carry = free_sweeps(
        adjoint_prev, viscosity, friction, ice_mask, (above, below), (packed, left, right),
        basal_velocity,
    )
    adjoint = add_response(
        got.reshape(-1, cols), devices, capacity, carry, adjoint
    )
    return (adjoint, gradient)


def solution(mesh):
    placed = (
        P(None, None, "gx", "gy"),
        P(None, "gx", "gy"),
        P("gx", "gy"),
        P(None, "gx", "gy"),
        P("gx", "gy"),
        P(("gx", "gy"), None, None),
        P(("gx", "gy"), None),
        P(("gx", "gy")),
    )

    return jax.shard_map(
        on_device,
        mesh=mesh,
        in_specs=placed,
        out_specs=(P(None, None, "gx", "gy"), P("gx", "gy")),
        check_vma=False,
    )
```

profile of v0, /device:TPU:15, one launch (start us, length us, event | category | flops | bytes accessed | tf_op | source)
XLA Modules:
  0.0 64.3 jit_solution(18415293604360224134)
XLA Ops:
  0.6 0.0 copy-start.4
  0.6 1.0 %copy-done.4 = bf16[1024,2,128]{2,1,0:T(2,128)(2,1)S(1)} copy-done((bf16[1024,2,128]{2,1,0:T(2,128)(2,1)S(1)}, bf16[1024,2,128]{2,1,0:T(2,128)(2,1)}, u32[]{:S(2)}) %copy-start.4) | copy-done | bytes 524312
  1.7 0.0 copy-start.6
  1.7 0.7 %copy-done.6 = s32[1024,1]{0,1:T(1,128)S(1)} copy-done((s32[1024,1]{0,1:T(1,128)S(1)}, s32[1024,1]{0,1:T(1,128)}, u32[]{:S(2)}) %copy-start.6) | copy-done | bytes 4120
  2.4 0.0 copy-start.7
  2.4 0.7 %copy-done.7 = s32[1024]{0:T(1024)S(1)} copy-done((s32[1024]{0:T(1024)S(1)}, s32[1024]{0:T(1024)}, u32[]{:S(2)}) %copy-start.7) | copy-done | bytes 4120
  3.0 1.7 %pack_blocks.1 = (bf16[2048,2,128]{2,1,0:T(2,128)(2,1)S(1)}, f32[32,128]{1,0:T(8,128)S(1)}, f32[32,128]{1,0:T(8,128)S(1)}) custom-call(s32[8,128]{1,0:T(8,128)S(1)} %bitcast.7, s32[8,128]{1,0:T(8,128)S(1)} %bitcast.8, bf16[1024,2,128]{2,1,0:T(2,128)(2,1)S(1)} %copy-done.4), custom_call_target="tpu_custom_call" | custom-call | tf_op jit(solution)/shard_map/pack_blocks/pallas_call | solution.py:596
  4.8 2.2 %bundle_blocks.1 = bf16[4864,128]{1,0:T(8,128)(2,1)} custom-call(bf16[4096,128]{1,0:T(8,128)(2,1)S(1)} %bitcast.6, f32[32,128]{1,0:T(8,128)S(1)} %get-tuple-element.11.keys, f32[32,128]{1,0:T(8,128)S(1)} %get-tuple-element.12.counts), custom_call_target="tpu_custom_call" | custom-call | tf_op jit(solution)/shard_map/bundle_blocks/pallas_call | solution.py:691
  7.0 6.2 %all-to-all-start = ((bf16[32,152,128]{2,1,0:T(8,128)(2,1)}), bf16[32,152,128]{2,1,0:T(8,128)(2,1)S(1)}, u32[]{:S(2)}, u32[]{:S(2)}) async-start(bf16[32,152,128]{2,1,0:T(8,128)(2,1)} %bitcast.3), calls=%async_computation | async-start | bytes 2490368 | tf_op jit(solution)/shard_map/all_to_all | solution.py:903
  13.2 0.0 copy-start
  13.2 0.0 copy-start.1
  13.3 0.0 copy-start.2
  13.3 0.0 copy-start.3
  13.3 2.0 %edge_rows.1 = (f32[184,128]{1,0:T(8,128)}, f32[184,128]{1,0:T(8,128)}) custom-call(f32[2,20,64,128]{3,2,1,0:T(8,128)} %adj.3, f32[2,20,64,128]{3,2,1,0:T(8,128)} %adj.3, f32[20,64,128]{2,1,0:T(8,128)} %eta_in.1, f32[20,64,128]{2,1,0:T(8,128)} %eta_in.1, f32[64,128]{1,0:T(8,128)} %fr.3, f32[64,128]{1,0:T(8,128)} %fr.3, s32[64,128]{1,0:T(8,128)} %ice.3, ...), custom_call_target="tpu_custom_call" | custom-call | tf_op jit(solution)/shard_map/edge_rows/pallas_call | solution.py:131
  15.2 0.0 copy-start.5
  15.2 1.4 %collective-permute-start = (f32[184,128]{1,0:T(8,128)}, f32[184,128]{1,0:T(8,128)S(1)}, u32[]{:S(2)}, u32[]{:S(2)}) collective-permute-start(f32[184,128]{1,0:T(8,128)} %get-tuple-element.13), channel_id=1, source_target_pairs={{0,8},{8,16},{16,24},{1,9},{9,17},{17,25},{2,10},{10,18},{18,26},{... | collective-permute-start | bytes 282632 | tf_op jit(solution)/shard_map/ppermute | solution.py:30
  16.7 4.0 %collective-permute-start.1 = (f32[184,128]{1,0:T(8,128)}, f32[184,128]{1,0:T(8,128)S(1)}, u32[]{:S(2)}, u32[]{:S(2)}) collective-permute-start(f32[184,128]{1,0:T(8,128)} %get-tuple-element.14), channel_id=1, source_target_pairs={{8,0},{16,8},{24,16},{9,1},{17,9},{25,17},{10,2},{18,10},{26,18},{... | collective-permute-start | bytes 282632 | tf_op jit(solution)/shard_map/ppermute | solution.py:35
  20.7 1.8 %collective-permute-done.above = f32[184,128]{1,0:T(8,128)S(1)} collective-permute-done((f32[184,128]{1,0:T(8,128)}, f32[184,128]{1,0:T(8,128)S(1)}, u32[]{:S(2)}, u32[]{:S(2)}) %collective-permute-start) | collective-permute-done | bytes 94240 | tf_op jit(solution)/shard_map/ppermute | solution.py:30
  22.4 1.5 %collective-permute-done.1.below = f32[184,128]{1,0:T(8,128)S(1)} collective-permute-done((f32[184,128]{1,0:T(8,128)}, f32[184,128]{1,0:T(8,128)S(1)}, u32[]{:S(2)}, u32[]{:S(2)}) %collective-permute-start.1) | collective-permute-done | bytes 94240 | tf_op jit(solution)/shard_map/ppermute | solution.py:35
  23.9 0.0 copy-done
  23.9 0.0 copy-done.1
  23.9 0.0 copy-done.2
  23.9 0.0 copy-done.3
  23.9 0.7 %edge_columns.1.packed = f32[3,72,128]{2,1,0:T(8,128)S(1)} custom-call(f32[2,20,64,128]{3,2,1,0:T(8,128)S(1)} %copy-done, f32[20,64,128]{2,1,0:T(8,128)S(1)} %copy-done.1, f32[64,128]{1,0:T(8,128)S(1)} %copy-done.2, s32[64,128]{1,0:T(8,128)S(1)} %copy-done.3, f32[184,128]{1,0:T(8,128)S(1)} %collective-permute-done.above, ...), custom_call_target="tpu_custom_call" | custom-call | tf_op jit(solution)/shard_map/edge_columns/pallas_call | solution.py:171
  24.7 3.4 %collective-permute-start.3 = (f32[3,72,128]{2,1,0:T(8,128)S(1)}, f32[3,72,128]{2,1,0:T(8,128)S(1)}, u32[]{:S(2)}, u32[]{:S(2)}) collective-permute-start(f32[3,72,128]{2,1,0:T(8,128)S(1)} %edge_columns.1.packed), channel_id=1, source_target_pairs={{1,0},{2,1},{3,2},{4,3},{5,4},{6,5},{7,6},{9,8},{10,9},{11,10},{12... | collective-permute-start | bytes 331784 | tf_op jit(solution)/shard_map/ppermute | solution.py:35
  28.1 3.3 %collective-permute-start.2 = (f32[3,72,128]{2,1,0:T(8,128)S(1)}, f32[3,72,128]{2,1,0:T(8,128)S(1)}, u32[]{:S(2)}, u32[]{:S(2)}) collective-permute-start(f32[3,72,128]{2,1,0:T(8,128)S(1)} %edge_columns.1.packed), channel_id=1, source_target_pairs={{0,1},{1,2},{2,3},{3,4},{4,5},{5,6},{6,7},{8,9},{9,10},{10,11},{11... | collective-permute-start | bytes 331784 | tf_op jit(solution)/shard_map/ppermute | solution.py:30
  31.4 12.0 %collective-permute-done.3.packed_right = f32[3,72,128]{2,1,0:T(8,128)S(1)} collective-permute-done((f32[3,72,128]{2,1,0:T(8,128)S(1)}, f32[3,72,128]{2,1,0:T(8,128)S(1)}, u32[]{:S(2)}, u32[]{:S(2)}) %collective-permute-start.3) | collective-permute-done | bytes 110624 | tf_op jit(solution)/shard_map/ppermute | solution.py:35
  43.4 0.0 collective-permute-done.2.packed_left
  43.4 0.0 copy-done.5
  43.4 17.4 %free_sweeps.1 = (f32[2,20,64,128]{3,2,1,0:T(8,128)}, f32[64,128]{1,0:T(8,128)}, f32[2,8,72,128]{3,2,1,0:T(8,128)S(1)}) custom-call(f32[2,20,64,128]{3,2,1,0:T(8,128)S(1)} %copy-done, f32[20,64,128]{2,1,0:T(8,128)S(1)} %copy-done.1, f32[64,128]{1,0:T(8,128)S(1)} %copy-done.2, s32[64,128]{1,0:T(8,128)S(1)} %copy-done.3, ...), custom_call_target="tpu_custom_call" | custom-call | flops 200000000 | bytes 8000000 | tf_op jit(solution)/shard_map/free_sweeps/pallas_call | solution.py:505
  60.8 0.0 all-to-all-done
  60.9 3.4 %add_response.1 = f32[2,20,64,128]{3,2,1,0:T(8,128)} custom-call(bf16[4864,128]{1,0:T(8,128)(2,1)S(1)} %bitcast.5, f32[2,8,72,128]{3,2,1,0:T(8,128)S(1)} %get-tuple-element.15.scale, f32[2,20,64,128]{3,2,1,0:T(8,128)} %get-tuple-element.16.adj_in), custom_call_target="tpu_custom_call", output_to_operand_aliasing={{}: (2, {})} | custom-call | tf_op jit(solution)/shard_map/add_response/pallas_call | solution.py:861
Async XLA Ops:
  0.6 1.0 %copy-start.4 = (bf16[1024,2,128]{2,1,0:T(2,128)(2,1)S(1)}, bf16[1024,2,128]{2,1,0:T(2,128)(2,1)}, u32[]{:S(2)}) copy-start(bf16[1024,2,128]{2,1,0:T(2,128)(2,1)} %misfit_in.1) | copy-start | bytes 1572868
  1.7 0.7 %copy-start.6 = (s32[1024,1]{0,1:T(1,128)S(1)}, s32[1024,1]{0,1:T(1,128)}, u32[]{:S(2)}) copy-start(s32[1024,1]{0,1:T(1,128)} %param.14) | copy-start | bytes 12292
  2.4 0.7 %copy-start.7 = (s32[1024]{0:T(1024)S(1)}, s32[1024]{0:T(1024)}, u32[]{:S(2)}) copy-start(s32[1024]{0:T(1024)} %param.15) | copy-start | bytes 12292
  7.0 53.9 %all-to-all-start = ((bf16[32,152,128]{2,1,0:T(8,128)(2,1)}), bf16[32,152,128]{2,1,0:T(8,128)(2,1)S(1)}, u32[]{:S(2)}, u32[]{:S(2)}) async-start(bf16[32,152,128]{2,1,0:T(8,128)(2,1)} %bitcast.3), calls=%async_computation | async-start | bytes 2490368 | tf_op jit(solution)/shard_map/all_to_all | solution.py:903
  13.2 10.7 %copy-start = (f32[2,20,64,128]{3,2,1,0:T(8,128)S(1)}, f32[2,20,64,128]{3,2,1,0:T(8,128)}, u32[]{:S(2)}) copy-start(f32[2,20,64,128]{3,2,1,0:T(8,128)} %adj.3) | copy-start | bytes 3932164
  13.2 10.6 %copy-start.1 = (f32[20,64,128]{2,1,0:T(8,128)S(1)}, f32[20,64,128]{2,1,0:T(8,128)}, u32[]{:S(2)}) copy-start(f32[20,64,128]{2,1,0:T(8,128)} %eta_in.1) | copy-start | bytes 1966084
  13.3 10.6 %copy-start.2 = (f32[64,128]{1,0:T(8,128)S(1)}, f32[64,128]{1,0:T(8,128)}, u32[]{:S(2)}) copy-start(f32[64,128]{1,0:T(8,128)} %fr.3) | copy-start | bytes 98308
  13.3 10.6 %copy-start.3 = (s32[64,128]{1,0:T(8,128)S(1)}, s32[64,128]{1,0:T(8,128)}, u32[]{:S(2)}) copy-start(s32[64,128]{1,0:T(8,128)} %ice.3) | copy-start | bytes 98308
  15.2 28.2 %copy-start.5 = (f32[2,64,128]{2,1,0:T(8,128)S(1)}, f32[2,64,128]{2,1,0:T(8,128)}, u32[]{:S(2)}) copy-start(f32[2,64,128]{2,1,0:T(8,128)} %basal_velocity.1) | copy-start | bytes 196612
  15.2 7.2 %collective-permute-start = (f32[184,128]{1,0:T(8,128)}, f32[184,128]{1,0:T(8,128)S(1)}, u32[]{:S(2)}, u32[]{:S(2)}) collective-permute-start(f32[184,128]{1,0:T(8,128)} %get-tuple-element.13), channel_id=1, source_target_pairs={{0,8},{8,16},{16,24},{1,9},{9,17},{17,25},{2,10},{10,18},{18,26},{... | collective-permute-start | bytes 282632 | tf_op jit(solution)/shard_map/ppermute | solution.py:30
  16.7 7.2 %collective-permute-start.1 = (f32[184,128]{1,0:T(8,128)}, f32[184,128]{1,0:T(8,128)S(1)}, u32[]{:S(2)}, u32[]{:S(2)}) collective-permute-start(f32[184,128]{1,0:T(8,128)} %get-tuple-element.14), channel_id=1, source_target_pairs={{8,0},{16,8},{24,16},{9,1},{17,9},{25,17},{10,2},{18,10},{26,18},{... | collective-permute-start | bytes 282632 | tf_op jit(solution)/shard_map/ppermute | solution.py:35
  24.7 18.8 %collective-permute-start.3 = (f32[3,72,128]{2,1,0:T(8,128)S(1)}, f32[3,72,128]{2,1,0:T(8,128)S(1)}, u32[]{:S(2)}, u32[]{:S(2)}) collective-permute-start(f32[3,72,128]{2,1,0:T(8,128)S(1)} %edge_columns.1.packed), channel_id=1, source_target_pairs={{1,0},{2,1},{3,2},{4,3},{5,4},{6,5},{7,6},{9,8},{10,9},{11,10},{12... | collective-permute-start | bytes 331784 | tf_op jit(solution)/shard_map/ppermute | solution.py:35
  28.1 15.4 %collective-permute-start.2 = (f32[3,72,128]{2,1,0:T(8,128)S(1)}, f32[3,72,128]{2,1,0:T(8,128)S(1)}, u32[]{:S(2)}, u32[]{:S(2)}) collective-permute-start(f32[3,72,128]{2,1,0:T(8,128)S(1)} %edge_columns.1.packed), channel_id=1, source_target_pairs={{0,1},{1,2},{2,3},{3,4},{4,5},{5,6},{6,7},{8,9},{9,10},{10,11},{11... | collective-permute-start | bytes 331784 | tf_op jit(solution)/shard_map/ppermute | solution.py:30
where the time goes:
time: 64.7 us; the launch traced here: 64.3 us
  Pallas kernels  27.5 us (43%)
  starting transfers between devices  18.4 us (28%)
  waiting for transfers between devices  15.2 us (23%)
  local copies, waits for them, and re-layouts  2.44 us (4%)
  between operations  0.74 us (1%)
    pallas_call x1, Pallas kernels, free_sweeps(): pl.pallas_call(functools.partial(sweep_kernel, layers), in_specs=vmem_spe...  17.4 us
    ppermute x2, waiting for transfers between devices, shift_down(): return lax.ppermute(array, axis, [(i + 1, i) for i in range(peers - 1)])  13.5 us
    ppermute x2, starting transfers between devices, shift_down(): return lax.ppermute(array, axis, [(i + 1, i) for i in range(peers - 1)])  7.39 us
    all_to_all x1, starting transfers between devices, on_device(): lax.all_to_all(sent.reshape(devices, -1, cols), ('gx', 'gy'), split_axis=...  6.24 us
    ppermute x2, starting transfers between devices, shift_up(): return lax.ppermute(array, axis, [(i, i + 1) for i in range(peers - 1)])  4.74 us
    pallas_call x1, Pallas kernels, add_response(): pl.pallas_call(functools.partial(response_kernel, devices, capacity), gri...  3.42 us
    unnamed x16, local copies, waits for them, and re-layouts  2.44 us
    pallas_call x1, Pallas kernels, bundle_blocks(): pl.pallas_call(functools.partial(bundle_kernel, devices, across, capacity...  2.2 us
  transfers between devices with their start and end apart: 5, of which 3 were waited for; matrix products, arithmetic and copies ran while one was open for 0% of the time, Pallas kernels for 31%

commit v1 on v0

--- a/solution.py
+++ b/solution.py
@@ -625,7 +625,12 @@
     return jnp.concatenate([high, values - high], axis=0)
 
 
-def bundle_kernel(devices, across, capacity, rows, slots, keys, counts, out, upper, lower, column):
+CHUNKS = 4
+
+
+def bundle_kernel(
+    devices, across, capacity, rows, slots, keys, counts, out_hbm, upper, lower, column, out, sems
+):
     lanes = slots.shape[1]
     span = 2 * capacity
     place = span + 2 * EXTRA
@@ -653,6 +658,7 @@
         if span < lanes:
             side = jnp.concatenate([side, jnp.zeros((8, lanes - span), F32)], axis=1)
         column[t] = side
+    copies = []
     zero_row = jnp.zeros((1, lanes), F32)
     zero_edge = jnp.zeros((8, lanes), F32)
     for t in range(devices):
@@ -682,6 +688,14 @@
         )
         extra = jnp.concatenate([head, above, below], axis=0).astype(BF16)
         out[place * t + span : place * (t + 1), :] = extra
+        if (t + 1) % (devices // CHUNKS) == 0:
+            chunk = t // (devices // CHUNKS)
+            part = pl.ds(chunk * place * (devices // CHUNKS), place * (devices // CHUNKS))
+            copy = pltpu.make_async_copy(out.at[part], out_hbm.at[part], sems.at[chunk])
+            copy.start()
+            copies.append(copy)
+    for copy in copies:
+        copy.wait()
 
 
 def bundle_blocks(slots, keys, counts, across, capacity, rows):
@@ -691,9 +705,15 @@
     return pl.pallas_call(
         functools.partial(bundle_kernel, devices, across, capacity, rows),
         in_specs=vmem_specs(3),
-        out_specs=pl.BlockSpec(memory_space=pltpu.VMEM),
+        out_specs=pl.BlockSpec(memory_space=pltpu.HBM),
         out_shape=jax.ShapeDtypeStruct((length, cols), BF16),
-        scratch_shapes=[edge, edge, edge],
+        scratch_shapes=[
+            edge,
+            edge,
+            edge,
+            pltpu.VMEM((length, cols), BF16),
+            pltpu.SemaphoreType.DMA((CHUNKS,)),
+        ],
         compiler_params=pltpu.CompilerParams(vmem_limit_bytes=8 << 20),
         name="bundle_blocks",
     )(slots, keys, counts)
@@ -837,7 +857,12 @@
                 put_tile(fields.at[turn, c, k + 1], r, new, tiles)
                 products[turn, c, k + 1, LEAD + 8 * r : LEAD + 8 * (r + 1), :] = e * new
 
-        for k in range(turn + 1):
+        for r in range(tiles - 1 if final else tiles):
+            e = tile_of(eta.at[turn + 1], r)
+            for c in range(2):
+                near = e * tile_of(fields.at[half, c, turn], r) + tile_of(products.at[half, c, turn], r)
+                put(c, turn, r, e, scale[c, turn, rows_of(r), :] * near)
+        for k in range(turn):
             drive = None
             if k == 0:
                 drive = lambda c, r, part=part: part * source[c, rows_of(r), :]

time: 64.7 us -> 64.4 us (level)
  transfers between devices with their start and end apart: 5 -> 5, of which waited for: 3 -> 3; matrix products, arithmetic and copies ran while one was open for 0% -> 0% of each run, Pallas kernels for 31% -> 32%
where the time goes in v1:
time: 64.4 us; the launch traced here: 63.9 us
  Pallas kernels  27.1 us (42%)
  starting transfers between devices  18.4 us (29%)
  waiting for transfers between devices  15.2 us (24%)
  local copies, waits for them, and re-layouts  2.44 us (4%)
  between operations  0.74 us (1%)
    pallas_call x1, Pallas kernels, free_sweeps(): pl.pallas_call(functools.partial(sweep_kernel, layers), in_specs=vmem_spe...  17.4 us
    ppermute x2, waiting for transfers between devices, shift_down(): return lax.ppermute(array, axis, [(i + 1, i) for i in range(peers - 1)])  13.5 us
    ppermute x2, starting transfers between devices, shift_down(): return lax.ppermute(array, axis, [(i + 1, i) for i in range(peers - 1)])  7.39 us
    all_to_all x1, starting transfers between devices, on_device(): lax.all_to_all(sent.reshape(devices, -1, cols), ('gx', 'gy'), split_axis=...  6.25 us
    ppermute x2, starting transfers between devices, shift_up(): return lax.ppermute(array, axis, [(i, i + 1) for i in range(peers - 1)])  4.74 us
    pallas_call x1, Pallas kernels, add_response(): pl.pallas_call(functools.partial(response_kernel, devices, capacity), gri...  3.22 us
    unnamed x16, local copies, waits for them, and re-layouts  2.44 us
    pallas_call x1, Pallas kernels, bundle_blocks(): pl.pallas_call(functools.partial(bundle_kernel, devices, across, capacity...  2.05 us
  transfers between devices with their start and end apart: 5, of which 3 were waited for; matrix products, arithmetic and copies ran while one was open for 0% of the time, Pallas kernels for 32%

profile of v1, /device:TPU:15, one launch (start us, length us, event | category | flops | bytes accessed | tf_op | source)
XLA Modules:
  0.0 63.9 jit_solution(4071127672730296979)
XLA Ops:
  0.6 0.0 copy-start.4
  0.6 1.0 %copy-done.4 = bf16[1024,2,128]{2,1,0:T(2,128)(2,1)S(1)} copy-done((bf16[1024,2,128]{2,1,0:T(2,128)(2,1)S(1)}, bf16[1024,2,128]{2,1,0:T(2,128)(2,1)}, u32[]{:S(2)}) %copy-start.4) | copy-done | bytes 524312
  1.7 0.0 copy-start.6
  1.7 0.7 %copy-done.6 = s32[1024,1]{0,1:T(1,128)S(1)} copy-done((s32[1024,1]{0,1:T(1,128)S(1)}, s32[1024,1]{0,1:T(1,128)}, u32[]{:S(2)}) %copy-start.6) | copy-done | bytes 4120
  2.4 0.0 copy-start.7
  2.4 0.7 %copy-done.7 = s32[1024]{0:T(1024)S(1)} copy-done((s32[1024]{0:T(1024)S(1)}, s32[1024]{0:T(1024)}, u32[]{:S(2)}) %copy-start.7) | copy-done | bytes 4120
  3.0 1.7 %pack_blocks.1 = (bf16[2048,2,128]{2,1,0:T(2,128)(2,1)S(1)}, f32[32,128]{1,0:T(8,128)S(1)}, f32[32,128]{1,0:T(8,128)S(1)}) custom-call(s32[8,128]{1,0:T(8,128)S(1)} %bitcast.7, s32[8,128]{1,0:T(8,128)S(1)} %bitcast.8, bf16[1024,2,128]{2,1,0:T(2,128)(2,1)S(1)} %copy-done.4), custom_call_target="tpu_custom_call" | custom-call | tf_op jit(solution)/shard_map/pack_blocks/pallas_call | solution.py:596
  4.8 2.1 %bundle_blocks.1 = bf16[4864,128]{1,0:T(8,128)(2,1)} custom-call(bf16[4096,128]{1,0:T(8,128)(2,1)S(1)} %bitcast.6, f32[32,128]{1,0:T(8,128)S(1)} %get-tuple-element.11.keys, f32[32,128]{1,0:T(8,128)S(1)} %get-tuple-element.12.counts), custom_call_target="tpu_custom_call" | custom-call | tf_op jit(solution)/shard_map/bundle_blocks/pallas_call | solution.py:705
  6.8 6.2 %all-to-all-start = ((bf16[32,152,128]{2,1,0:T(8,128)(2,1)}), bf16[32,152,128]{2,1,0:T(8,128)(2,1)S(1)}, u32[]{:S(2)}, u32[]{:S(2)}) async-start(bf16[32,152,128]{2,1,0:T(8,128)(2,1)} %bitcast.3), calls=%async_computation | async-start | bytes 2490368 | tf_op jit(solution)/shard_map/all_to_all | solution.py:928
  13.1 0.0 copy-start
  13.1 0.0 copy-start.1
  13.1 0.0 copy-start.2
  13.1 0.0 copy-start.3
  13.1 2.0 %edge_rows.1 = (f32[184,128]{1,0:T(8,128)}, f32[184,128]{1,0:T(8,128)}) custom-call(f32[2,20,64,128]{3,2,1,0:T(8,128)} %adj.3, f32[2,20,64,128]{3,2,1,0:T(8,128)} %adj.3, f32[20,64,128]{2,1,0:T(8,128)} %eta_in.1, f32[20,64,128]{2,1,0:T(8,128)} %eta_in.1, f32[64,128]{1,0:T(8,128)} %fr.3, f32[64,128]{1,0:T(8,128)} %fr.3, s32[64,128]{1,0:T(8,128)} %ice.3, ...), custom_call_target="tpu_custom_call" | custom-call | tf_op jit(solution)/shard_map/edge_rows/pallas_call | solution.py:131
  15.1 0.0 copy-start.5
  15.1 1.4 %collective-permute-start = (f32[184,128]{1,0:T(8,128)}, f32[184,128]{1,0:T(8,128)S(1)}, u32[]{:S(2)}, u32[]{:S(2)}) collective-permute-start(f32[184,128]{1,0:T(8,128)} %get-tuple-element.13), channel_id=1, source_target_pairs={{0,8},{8,16},{16,24},{1,9},{9,17},{17,25},{2,10},{10,18},{18,26},{... | collective-permute-start | bytes 282632 | tf_op jit(solution)/shard_map/ppermute | solution.py:30
  16.5 4.0 %collective-permute-start.1 = (f32[184,128]{1,0:T(8,128)}, f32[184,128]{1,0:T(8,128)S(1)}, u32[]{:S(2)}, u32[]{:S(2)}) collective-permute-start(f32[184,128]{1,0:T(8,128)} %get-tuple-element.14), channel_id=1, source_target_pairs={{8,0},{16,8},{24,16},{9,1},{17,9},{25,17},{10,2},{18,10},{26,18},{... | collective-permute-start | bytes 282632 | tf_op jit(solution)/shard_map/ppermute | solution.py:35
  20.5 1.8 %collective-permute-done.above = f32[184,128]{1,0:T(8,128)S(1)} collective-permute-done((f32[184,128]{1,0:T(8,128)}, f32[184,128]{1,0:T(8,128)S(1)}, u32[]{:S(2)}, u32[]{:S(2)}) %collective-permute-start) | collective-permute-done | bytes 94240 | tf_op jit(solution)/shard_map/ppermute | solution.py:30
  22.3 1.5 %collective-permute-done.1.below = f32[184,128]{1,0:T(8,128)S(1)} collective-permute-done((f32[184,128]{1,0:T(8,128)}, f32[184,128]{1,0:T(8,128)S(1)}, u32[]{:S(2)}, u32[]{:S(2)}) %collective-permute-start.1) | collective-permute-done | bytes 94240 | tf_op jit(solution)/shard_map/ppermute | solution.py:35
  23.7 0.0 copy-done
  23.8 0.0 copy-done.1
  23.8 0.0 copy-done.2
  23.8 0.0 copy-done.3
  23.8 0.7 %edge_columns.1.packed = f32[3,72,128]{2,1,0:T(8,128)S(1)} custom-call(f32[2,20,64,128]{3,2,1,0:T(8,128)S(1)} %copy-done, f32[20,64,128]{2,1,0:T(8,128)S(1)} %copy-done.1, f32[64,128]{1,0:T(8,128)S(1)} %copy-done.2, s32[64,128]{1,0:T(8,128)S(1)} %copy-done.3, f32[184,128]{1,0:T(8,128)S(1)} %collective-permute-done.above, ...), custom_call_target="tpu_custom_call" | custom-call | tf_op jit(solution)/shard_map/edge_columns/pallas_call | solution.py:171
  24.5 3.4 %collective-permute-start.3 = (f32[3,72,128]{2,1,0:T(8,128)S(1)}, f32[3,72,128]{2,1,0:T(8,128)S(1)}, u32[]{:S(2)}, u32[]{:S(2)}) collective-permute-start(f32[3,72,128]{2,1,0:T(8,128)S(1)} %edge_columns.1.packed), channel_id=1, source_target_pairs={{1,0},{2,1},{3,2},{4,3},{5,4},{6,5},{7,6},{9,8},{10,9},{11,10},{12... | collective-permute-start | bytes 331784 | tf_op jit(solution)/shard_map/ppermute | solution.py:35
  27.9 3.3 %collective-permute-start.2 = (f32[3,72,128]{2,1,0:T(8,128)S(1)}, f32[3,72,128]{2,1,0:T(8,128)S(1)}, u32[]{:S(2)}, u32[]{:S(2)}) collective-permute-start(f32[3,72,128]{2,1,0:T(8,128)S(1)} %edge_columns.1.packed), channel_id=1, source_target_pairs={{0,1},{1,2},{2,3},{3,4},{4,5},{5,6},{6,7},{8,9},{9,10},{10,11},{11... | collective-permute-start | bytes 331784 | tf_op jit(solution)/shard_map/ppermute | solution.py:30
  31.3 12.0 %collective-permute-done.3.packed_right = f32[3,72,128]{2,1,0:T(8,128)S(1)} collective-permute-done((f32[3,72,128]{2,1,0:T(8,128)S(1)}, f32[3,72,128]{2,1,0:T(8,128)S(1)}, u32[]{:S(2)}, u32[]{:S(2)}) %collective-permute-start.3) | collective-permute-done | bytes 110624 | tf_op jit(solution)/shard_map/ppermute | solution.py:35
  43.3 0.0 collective-permute-done.2.packed_left
  43.3 0.0 copy-done.5
  43.3 17.4 %free_sweeps.1 = (f32[2,20,64,128]{3,2,1,0:T(8,128)}, f32[64,128]{1,0:T(8,128)}, f32[2,8,72,128]{3,2,1,0:T(8,128)S(1)}) custom-call(f32[2,20,64,128]{3,2,1,0:T(8,128)S(1)} %copy-done, f32[20,64,128]{2,1,0:T(8,128)S(1)} %copy-done.1, f32[64,128]{1,0:T(8,128)S(1)} %copy-done.2, s32[64,128]{1,0:T(8,128)S(1)} %copy-done.3, ...), custom_call_target="tpu_custom_call" | custom-call | flops 200000000 | bytes 8000000 | tf_op jit(solution)/shard_map/free_sweeps/pallas_call | solution.py:505
  60.7 0.0 all-to-all-done
  60.7 3.2 %add_response.1 = f32[2,20,64,128]{3,2,1,0:T(8,128)} custom-call(bf16[4864,128]{1,0:T(8,128)(2,1)S(1)} %bitcast.5, f32[2,8,72,128]{3,2,1,0:T(8,128)S(1)} %get-tuple-element.15.scale, f32[2,20,64,128]{3,2,1,0:T(8,128)} %get-tuple-element.16.adj_in), custom_call_target="tpu_custom_call", output_to_operand_aliasing={{}: (2, {})} | custom-call | tf_op jit(solution)/shard_map/add_response/pallas_call | solution.py:886
Async XLA Ops:
  0.6 1.0 %copy-start.4 = (bf16[1024,2,128]{2,1,0:T(2,128)(2,1)S(1)}, bf16[1024,2,128]{2,1,0:T(2,128)(2,1)}, u32[]{:S(2)}) copy-start(bf16[1024,2,128]{2,1,0:T(2,128)(2,1)} %misfit_in.1) | copy-start | bytes 1572868
  1.7 0.7 %copy-start.6 = (s32[1024,1]{0,1:T(1,128)S(1)}, s32[1024,1]{0,1:T(1,128)}, u32[]{:S(2)}) copy-start(s32[1024,1]{0,1:T(1,128)} %param.14) | copy-start | bytes 12292
  2.4 0.7 %copy-start.7 = (s32[1024]{0:T(1024)S(1)}, s32[1024]{0:T(1024)}, u32[]{:S(2)}) copy-start(s32[1024]{0:T(1024)} %param.15) | copy-start | bytes 12292
  6.8 53.9 %all-to-all-start = ((bf16[32,152,128]{2,1,0:T(8,128)(2,1)}), bf16[32,152,128]{2,1,0:T(8,128)(2,1)S(1)}, u32[]{:S(2)}, u32[]{:S(2)}) async-start(bf16[32,152,128]{2,1,0:T(8,128)(2,1)} %bitcast.3), calls=%async_computation | async-start | bytes 2490368 | tf_op jit(solution)/shard_map/all_to_all | solution.py:928
  13.1 10.7 %copy-start = (f32[2,20,64,128]{3,2,1,0:T(8,128)S(1)}, f32[2,20,64,128]{3,2,1,0:T(8,128)}, u32[]{:S(2)}) copy-start(f32[2,20,64,128]{3,2,1,0:T(8,128)} %adj.3) | copy-start | bytes 3932164
  13.1 10.6 %copy-start.1 = (f32[20,64,128]{2,1,0:T(8,128)S(1)}, f32[20,64,128]{2,1,0:T(8,128)}, u32[]{:S(2)}) copy-start(f32[20,64,128]{2,1,0:T(8,128)} %eta_in.1) | copy-start | bytes 1966084
  13.1 10.6 %copy-start.2 = (f32[64,128]{1,0:T(8,128)S(1)}, f32[64,128]{1,0:T(8,128)}, u32[]{:S(2)}) copy-start(f32[64,128]{1,0:T(8,128)} %fr.3) | copy-start | bytes 98308
  13.1 10.6 %copy-start.3 = (s32[64,128]{1,0:T(8,128)S(1)}, s32[64,128]{1,0:T(8,128)}, u32[]{:S(2)}) copy-start(s32[64,128]{1,0:T(8,128)} %ice.3) | copy-start | bytes 98308
  15.1 28.2 %copy-start.5 = (f32[2,64,128]{2,1,0:T(8,128)S(1)}, f32[2,64,128]{2,1,0:T(8,128)}, u32[]{:S(2)}) copy-start(f32[2,64,128]{2,1,0:T(8,128)} %basal_velocity.1) | copy-start | bytes 196612
  15.1 7.2 %collective-permute-start = (f32[184,128]{1,0:T(8,128)}, f32[184,128]{1,0:T(8,128)S(1)}, u32[]{:S(2)}, u32[]{:S(2)}) collective-permute-start(f32[184,128]{1,0:T(8,128)} %get-tuple-element.13), channel_id=1, source_target_pairs={{0,8},{8,16},{16,24},{1,9},{9,17},{17,25},{2,10},{10,18},{18,26},{... | collective-permute-start | bytes 282632 | tf_op jit(solution)/shard_map/ppermute | solution.py:30
  16.5 7.2 %collective-permute-start.1 = (f32[184,128]{1,0:T(8,128)}, f32[184,128]{1,0:T(8,128)S(1)}, u32[]{:S(2)}, u32[]{:S(2)}) collective-permute-start(f32[184,128]{1,0:T(8,128)} %get-tuple-element.14), channel_id=1, source_target_pairs={{8,0},{16,8},{24,16},{9,1},{17,9},{25,17},{10,2},{18,10},{26,18},{... | collective-permute-start | bytes 282632 | tf_op jit(solution)/shard_map/ppermute | solution.py:35
  24.5 18.8 %collective-permute-start.3 = (f32[3,72,128]{2,1,0:T(8,128)S(1)}, f32[3,72,128]{2,1,0:T(8,128)S(1)}, u32[]{:S(2)}, u32[]{:S(2)}) collective-permute-start(f32[3,72,128]{2,1,0:T(8,128)S(1)} %edge_columns.1.packed), channel_id=1, source_target_pairs={{1,0},{2,1},{3,2},{4,3},{5,4},{6,5},{7,6},{9,8},{10,9},{11,10},{12... | collective-permute-start | bytes 331784 | tf_op jit(solution)/shard_map/ppermute | solution.py:35
  27.9 15.4 %collective-permute-start.2 = (f32[3,72,128]{2,1,0:T(8,128)S(1)}, f32[3,72,128]{2,1,0:T(8,128)S(1)}, u32[]{:S(2)}, u32[]{:S(2)}) collective-permute-start(f32[3,72,128]{2,1,0:T(8,128)S(1)} %edge_columns.1.packed), channel_id=1, source_target_pairs={{0,1},{1,2},{2,3},{3,4},{4,5},{5,6},{6,7},{8,9},{9,10},{10,11},{11... | collective-permute-start | bytes 331784 | tf_op jit(solution)/shard_map/ppermute | solution.py:30
